TPU v7x, 512 devices: a whole 4x4x16 slice. The times are simulated.
512 devices in a mesh: dp: 32 (over z, core), tensor: 16 (over y, x).
Axes of the slice: x: 4, y: 4, z: 16, core: 2. Of those that a mesh axis runs over, the one named last changes fastest.
Arguments:
- dout: bfloat16 [12288, 5120], P(('dp', 'tensor')), may hold values from -0.75 to 0.75
- attn_ctx: bfloat16 [12288, 5120], P('dp', 'tensor'), may hold values from -6 to 6
- mlp_hidden: bfloat16 [12288, 13824], P('dp', 'tensor'), may hold values from -6 to 6
- w_out: bfloat16 [5120, 5120], P('tensor', 'dp'), may hold values from -0.078125 to 0.078125
- w_down: bfloat16 [13824, 5120], P('tensor', 'dp'), may hold values from -0.0546875 to 0.0546875
- head_logits: float32 [40], replicated, may hold values from -2 to 3
- unit_logits: float32 [13824], P('tensor'), may hold values from -2 to 3
- head_noise: float32 [40], replicated, may hold values from 0.001 to 0.999
- unit_noise: float32 [13824], P('tensor'), may hold values from 0.001 to 0.999
- linear_mult: float32 [1], replicated, may hold values from 100 to 300
- square_mult: float32 [1], replicated, may hold values from 1 to 4
- target: float32 [1], replicated, may hold values from 40 to 70
Outputs:
- ctx_grad: bfloat16 [12288, 5120], P('dp', 'tensor')
- hidden_grad: bfloat16 [12288, 13824], P('dp', 'tensor')
- head_grad: float32 [40], replicated
- unit_grad: float32 [13824], P('tensor')
All inputs are finite; a program needn't handle non-finite values.
Results may differ from a plain program's by a relative error of at most 0.001.
Values may be sent and summed in bfloat16 or wider, within the bound.
No kernel may reach another device: no remote copies, remote signals or barrier semaphores. Data moves between devices by JAX's collectives and lax.ppermute only.
A program may use at most 64 MiB of HBM per device.

v0:
```python
import jax
import jax.numpy as jnp
from jax import lax
from jax.sharding import PartitionSpec as P

H = 40
HEAD = 128
FF = 13824
low_end = -0.1
high_end = 1.1
temper = 2.0 / 3.0


def concrete(logits, noise):
    shape_s = jax.nn.sigmoid((jnp.log(noise) - jnp.log(1.0 - noise) + logits) / temper)
    stretched = shape_s * (high_end - low_end) + low_end
    gate = jnp.clip(stretched, 0.0, 1.0)
    inside = jnp.logical_and(stretched > 0.0, stretched < 1.0)
    slope = jnp.where(
        inside, (high_end - low_end) / temper * shape_s * (1.0 - shape_s), 0.0 * shape_s
    )
    return (gate, slope)


def open_prob(logits):
    return jax.nn.sigmoid(logits - temper * jnp.log(-low_end / high_end))


def local(
    dout,
    attn_ctx,
    mlp_hidden,
    w_out,
    w_down,
    head_logits,
    unit_logits,
    head_noise,
    unit_noise,
    linear_mult,
    square_mult,
    target,
):
    head_gate, head_slope = concrete(head_logits, head_noise)
    unit_gate, unit_slope = concrete(unit_logits, unit_noise)
    col_count = attn_ctx.shape[1]
    head_total = head_logits.shape[0]
    tensor_index = lax.axis_index("tensor")
    columns = tensor_index * col_count + lax.iota(jnp.int32, col_count)
    owner = columns // HEAD
    member = (owner[:, None] == lax.iota(jnp.int32, head_total)[None, :]).astype(jnp.float32)
    col_gate = jnp.dot(member, head_gate, precision=lax.Precision.HIGHEST)
    full_rows = lax.all_gather(dout, "tensor", axis=0, tiled=True)
    dims = (((1,), (1,)), ((), ()))

    def contract(piece):
        return lax.dot_general(full_rows, piece, dims, preferred_element_type=jnp.float32)

    ctx_pre = contract(lax.all_gather(w_out, "dp", axis=1, tiled=True))
    hid_pre = contract(lax.all_gather(w_down, "dp", axis=1, tiled=True))
    ctx_grad = (ctx_pre * col_gate[None, :]).astype(jnp.bfloat16)
    hidden_grad = (hid_pre * unit_gate[None, :]).astype(jnp.bfloat16)
    col_part = jnp.sum(attn_ctx.astype(jnp.float32) * ctx_pre, axis=0)
    unit_part = jnp.sum(mlp_hidden.astype(jnp.float32) * hid_pre, axis=0)
    head_part = jnp.dot(col_part, member, precision=lax.Precision.HIGHEST)
    p_head = open_prob(head_logits)
    p_unit = open_prob(unit_logits)
    local_mass = jnp.sum(p_unit)
    unit_data = lax.psum(unit_part, "dp")
    head_data = lax.psum(head_part, ("dp", "tensor"))
    unit_mass = lax.psum(local_mass, "tensor")
    denom = 4.0 * HEAD * H + 3.0 * FF
    size = 100.0 * (4.0 * HEAD * jnp.sum(p_head) + 3.0 * unit_mass) / denom
    factor = linear_mult[0] + 2.0 * square_mult[0] * (size - target[0])
    head_grad = head_data * head_slope + factor * (400.0 * HEAD / denom) * p_head * (1.0 - p_head)
    unit_grad = unit_data * unit_slope + factor * (300.0 / denom) * p_unit * (1.0 - p_unit)
    return (ctx_grad, hidden_grad, head_grad, unit_grad)


def solution(mesh):
    placed = (
        P(("dp", "tensor"), None),
        P("dp", "tensor"),
        P("dp", "tensor"),
        P("tensor", "dp"),
        P("tensor", "dp"),
        P(),
        P("tensor"),
        P(),
        P("tensor"),
        P(),
        P(),
        P(),
    )
    return jax.shard_map(
        local,
        mesh=mesh,
        in_specs=placed,
        out_specs=(P("dp", "tensor"), P("dp", "tensor"), P(), P("tensor")),
        check_vma=False,
    )
```

profile of v0, /device:TPU:1, one launch (start us, length us, event | category | flops | bytes accessed | tf_op | source)
XLA Modules:
  0.0 329.6 jit_solution(5489138382124432926)
XLA Ops:
  7.2 0.0 all-gather.6.cloned.1.call-start
  7.2 0.7 all-gather.6.cloned.1.call-update
  7.9 0.0 all-gather.4.cloned.1.call-start
  7.9 0.7 all-gather.4.cloned.1.call-update
  8.6 0.0 all-gather.8.cloned.1.call-start
  8.7 0.7 all-gather.8.cloned.1.call-update
  9.4 1.3 fusion.2
  10.7 34.9 %psum.22 = f32[]{:T(128)} all-reduce(f32[]{:T(128)} %get-tuple-element.11), channel_id=1, replica_groups=mesh['dp'=32,'tensor'=16] {'tensor'}, use_global_device_ids=true, to_apply=%region_4.5 | all-reduce | flops 1 | bytes 8 | tf_op jit(solution)/shard_map/psum | solution.py:70
  48.2 1.3 fusion.17
  50.1 0.0 copy-start.2
  50.1 0.0 copy-start.3
  50.2 0.0 copy-start.4
  50.2 38.7 %all-gather.6.cloned.1.call-done = bf16[320,5120]{0,1:T(8,128)(2,1)} async-done(((bf16[320,160]{0,1:T(8,128)(2,1)}), bf16[320,5120]{0,1:T(8,128)(2,1)}) %all-gather.6.cloned.1.call-update) | async-done | bytes 3276816 | tf_op jit(solution)/shard_map/all_gather | solution.py:58
  88.8 65.0 %all-gather.4.cloned.1.call-done = bf16[384,5120]{1,0:T(8,128)(2,1)} async-done(((bf16[24,5120]{1,0:T(8,128)(2,1)}), bf16[384,5120]{1,0:T(8,128)(2,1)}) %all-gather.4.cloned.1.call-update) | async-done | bytes 3932176 | tf_op jit(solution)/shard_map/all_gather | solution.py:52
  153.9 5.3 %multiply_reduce_fusion.1 = (f32[320]{0:T(512)S(1)}, f32[384,320]{0,1:T(8,128)S(1)}) fusion(bf16[384,320]{0,1:T(8,128)(2,1)} %param.13, bf16[384,5120]{1,0:T(8,128)(2,1)} %all-gather.4.cloned.1.call-done, bf16[320,5120]{0,1:T(8,128)(2,1)} %all-gather.6.cloned.1.call-done), kind=kOutput, calls=%fused_computation.4 | convolution fusion | flops 1258659584 | bytes 7947520 | tf_op jit(solution)/shard_map/dot_general | solution.py:56
  159.2 0.2 convolution_bitcast_fusion
  159.5 105.0 %psum.21 = f32[40]{0:T(128)S(1)} all-reduce(f32[40]{0:T(128)S(1)} %convolution_bitcast_fusion), channel_id=1, replica_groups=mesh['dp'=32,'tensor'=16] {'dp','tensor'}, use_global_device_ids=true, to_apply=%region_1.2 | all-reduce | flops 40 | bytes 320 | tf_op jit(solution)/shard_map/psum | solution.py:69
  264.5 0.0 copy-done.2
  264.5 0.0 copy-done.3
  264.5 0.5 multiply_add_fusion.2
  265.0 0.3 convolution_reduce_fusion
  265.3 0.8 multiply_convert_fusion.1
  266.1 0.0 all-gather.8.cloned.1.call-done
  266.2 0.0 copy-done.4
  266.2 0.0 copy-start
  266.2 0.0 copy-start.1
  266.2 10.5 %multiply_reduce_fusion = (f32[864]{0:T(1024)S(1)}, bf16[384,864]{0,1:T(8,128)(2,1)}) fusion(bf16[384,864]{0,1:T(8,128)(2,1)S(1)} %copy-done.4, f32[864]{0:T(1024)S(1)} %get-tuple-element.10, bf16[384,5120]{1,0:T(8,128)(2,1)} %all-gather.4.cloned.1.call-done, bf16[864,5120]{0,1:T(8,128)(2,1)} %all-gather.8.cloned.1.call-done), kind=kOutput, calls=%fused_computation | convolution fusion | flops 3399044352 | bytes 14113536 | tf_op jit(solution)/shard_map/dot_general | solution.py:56
  276.7 45.8 %psum.23 = f32[864]{0:T(1024)S(1)} all-reduce(f32[864]{0:T(1024)S(1)} %get-tuple-element.8), channel_id=1, replica_groups=mesh['dp'=32,'tensor'=16] {'dp'}, use_global_device_ids=true, to_apply=%region_6.7 | all-reduce | flops 864 | bytes 6912 | tf_op jit(solution)/shard_map/psum | solution.py:68
  322.5 0.0 copy-done
  322.5 0.0 copy-done.1
  322.5 0.6 multiply_add_fusion
  (2 shorter events, 0.0 us)
Async XLA Ops:
  7.2 81.7 %all-gather.6.cloned.1.call-start = ((), (), s32[]{:S(2)}) async-start(), calls=%async_computation.1 | async-start | bytes 4055040 | tf_op jit(solution)/shard_map/all_gather | solution.py:58
  7.9 146.0 %all-gather.4.cloned.1.call-start = ((), (), s32[]{:S(2)}) async-start(), calls=%async_computation | async-start | bytes 4177920 | tf_op jit(solution)/shard_map/all_gather | solution.py:52
  8.6 257.5 %all-gather.8.cloned.1.call-start = ((), (), s32[]{:S(2)}) async-start(), calls=%async_computation.2 | async-start | bytes 9461760 | tf_op jit(solution)/shard_map/all_gather | solution.py:59
  50.1 214.4 %copy-start.2 = (f32[40]{0:T(128)S(1)}, f32[40]{0:T(128)}, u32[]{:S(2)}) copy-start(f32[40]{0:T(128)} %param.17) | copy-start | bytes 484
  50.1 214.4 %copy-start.3 = (f32[40]{0:T(128)S(1)}, f32[40]{0:T(128)}, u32[]{:S(2)}) copy-start(f32[40]{0:T(128)} %param.19) | copy-start | bytes 484
  50.2 216.0 %copy-start.4 = (bf16[384,864]{0,1:T(8,128)(2,1)S(1)}, bf16[384,864]{0,1:T(8,128)(2,1)}, u32[]{:S(2)}) copy-start(bf16[384,864]{0,1:T(8,128)(2,1)} %param.14) | copy-start | bytes 1990660
  266.2 56.3 %copy-start = (f32[864]{0:T(1024)S(1)}, f32[864]{0:T(1024)}, u32[]{:S(2)}) copy-start(f32[864]{0:T(1024)} %param.18) | copy-start | bytes 10372
  266.2 56.3 %copy-start.1 = (f32[864]{0:T(1024)S(1)}, f32[864]{0:T(1024)}, u32[]{:S(2)}) copy-start(f32[864]{0:T(1024)} %param.20) | copy-start | bytes 10372
Sparse Core Ops, SparseCore 0:
  10.1 78.6 all-gather.5
  91.8 61.9 all-gather.3
  156.0 80.5 all-gather.7
where the time goes:
time: 330 us
  blocking collectives  186 us (56%)
  waiting for transfers between devices  106 us (32%)
  between operations  17.1 us (5%)
  matrix products  16.4 us (5%)
  other arithmetic  4.6 us (1%)
    psum x1, blocking collectives, local(): head_data = lax.psum(head_part, ('dp', 'tensor'))  105 us
    all_gather x1, waiting for transfers between devices, local(): full_rows = lax.all_gather(dout, 'tensor', axis=0, tiled=True)  65 us
    psum x1, blocking collectives, local(): unit_data = lax.psum(unit_part, 'dp')  45.8 us
    all_gather x1, waiting for transfers between devices, local(): ctx_pre = contract(lax.all_gather(w_out, 'dp', axis=1, tiled=True))  38.7 us
    psum x1, blocking collectives, local(): unit_mass = lax.psum(local_mass, 'tensor')  34.9 us
    dot_general x2, matrix products, contract(): lax.dot_general(full_rows, piece, dims, preferred_element_type=jnp.float32)  15.9 us
  transfers between devices with their start and end apart: 3, of which 2 were waited for; matrix products, arithmetic and copies ran while one was open for 3% of the time, Pallas kernels for 0%

commit v1 on v0

--- a/solution.py
+++ b/solution.py
@@ -55,7 +55,11 @@
     def contract(piece):
         return lax.dot_general(full_rows, piece, dims, preferred_element_type=jnp.float32)
 
-    ctx_pre = contract(lax.all_gather(w_out, "dp", axis=1, tiled=True))
+    ctx_pre = contract(
+        jnp.concatenate(
+            lax.all_to_all(jnp.stack([w_out] * lax.axis_size("dp")), "dp", 0, 0), axis=1
+        )
+    )
     hid_pre = contract(lax.all_gather(w_down, "dp", axis=1, tiled=True))
     ctx_grad = (ctx_pre * col_gate[None, :]).astype(jnp.bfloat16)
     hidden_grad = (hid_pre * unit_gate[None, :]).astype(jnp.bfloat16)

time: 330 us -> 408 us (1.24)
  waiting for transfers between devices: 106 us -> 166 us
  starting transfers between devices: 0.11 us -> 17 us
    all_to_all x0 -> x1, waiting for transfers between devices: none -> 152 us  [local(): lax.all_to_all(jnp.stack([w_out] * lax.axis_size('dp')), 'dp', 0, 0)]
    all_gather x1, waiting for transfers between devices: 65 us -> 11.9 us  [local(): full_rows = lax.all_gather(dout, 'tensor', axis=0, tiled=True)]
    all_gather x1 -> x0, waiting for transfers between devices: 38.7 us -> none  [local(): ctx_pre = contract(lax.all_gather(w_out, 'dp', axis=1, tiled=True))]
    all_to_all x0 -> x1, starting transfers between devices: none -> 16.9 us  [local(): lax.all_to_all(jnp.stack([w_out] * lax.axis_size('dp')), 'dp', 0, 0)]
where the time goes in v1:
time: 408 us
  blocking collectives  185 us (45%)
  waiting for transfers between devices  166 us (41%)
  between operations  17.4 us (4%)
  starting transfers between devices  17 us (4%)
  matrix products  16.6 us (4%)
    all_to_all x1, waiting for transfers between devices, local(): lax.all_to_all(jnp.stack([w_out] * lax.axis_size('dp')), 'dp', 0, 0)  152 us
    psum x1, blocking collectives, local(): head_data = lax.psum(head_part, ('dp', 'tensor'))  102 us
    psum x1, blocking collectives, local(): unit_data = lax.psum(unit_part, 'dp')  46.1 us
    psum x1, blocking collectives, local(): unit_mass = lax.psum(local_mass, 'tensor')  36.5 us
    all_to_all x1, starting transfers between devices, local(): lax.all_to_all(jnp.stack([w_out] * lax.axis_size('dp')), 'dp', 0, 0)  16.9 us
    dot_general x2, matrix products, contract(): lax.dot_general(full_rows, piece, dims, preferred_element_type=jnp.float32)  16 us
    all_gather x1, waiting for transfers between devices, local(): full_rows = lax.all_gather(dout, 'tensor', axis=0, tiled=True)  11.9 us
  transfers between devices with their start and end apart: 3, of which 2 were waited for; matrix products, arithmetic and copies ran while one was open for 3% of the time, Pallas kernels for 0%

profile of v1, /device:TPU:1, one launch (start us, length us, event | category | flops | bytes accessed | tf_op | source)
XLA Modules:
  0.0 407.8 jit_solution(17957573160274445598)
XLA Ops:
  7.2 0.0 all-gather.3.cloned.1.call-start
  7.2 0.7 all-gather.3.cloned.1.call-update
  7.9 0.0 all-gather.5.cloned.1.call-start
  7.9 0.7 all-gather.5.cloned.1.call-update
  8.6 3.1 stack.2
  11.7 0.0 copy-start
  11.7 0.0 copy-start.1
  11.7 0.0 copy-start.2
  11.7 0.0 copy-start.5
  11.7 16.9 %all-to-all-start = ((bf16[32,320,160]{1,2,0:T(8,128)(2,1)}), bf16[32,320,160]{1,2,0:T(8,128)(2,1)}, u32[]{:S(2)}, u32[]{:S(2)}) async-start(bf16[32,320,160]{1,2,0:T(8,128)(2,1)} %stack.2), calls=%async_computation | async-start | bytes 7864320 | tf_op jit(solution)/shard_map/all_to_all | solution.py:60
  28.7 0.0 copy-done
  28.7 0.0 copy-done.1
  28.7 0.6 fusion.2
  29.3 36.5 %psum.22 = f32[]{:T(128)} all-reduce(f32[]{:T(128)} %get-tuple-element.11), channel_id=1, replica_groups=mesh['dp'=32,'tensor'=16] {'tensor'}, use_global_device_ids=true, to_apply=%region_4.5 | all-reduce | flops 1 | bytes 8 | tf_op jit(solution)/shard_map/psum | solution.py:74
  67.8 0.0 copy-done.2
  67.8 0.6 fusion.17
  69.8 11.9 %all-gather.3.cloned.1.call-done = bf16[384,5120]{1,0:T(8,128)(2,1)} async-done(((bf16[24,5120]{1,0:T(8,128)(2,1)}), bf16[384,5120]{1,0:T(8,128)(2,1)}) %all-gather.3.cloned.1.call-update) | async-done | bytes 3932176 | tf_op jit(solution)/shard_map/all_gather | solution.py:52
  81.6 152.3 %all-to-all-done = bf16[32,320,160]{1,2,0:T(8,128)(2,1)} async-done(((bf16[32,320,160]{1,2,0:T(8,128)(2,1)}), bf16[32,320,160]{1,2,0:T(8,128)(2,1)}, u32[]{:S(2)}, u32[]{:S(2)}) %all-to-all-start) | async-done | bytes 3276832 | tf_op jit(solution)/shard_map/all_to_all | solution.py:60
  234.0 0.0 copy-done.5
  234.0 0.0 copy-start.3
  234.0 0.0 copy-start.4
  234.0 5.6 %multiply_reduce_fusion.1 = (f32[320]{0:T(512)S(1)}, f32[384,320]{0,1:T(8,128)S(1)}) fusion(bf16[384,320]{0,1:T(8,128)(2,1)S(1)} %copy-done.5, bf16[384,5120]{1,0:T(8,128)(2,1)} %all-gather.3.cloned.1.call-done, bf16[320,5120]{0,1:T(8,128)(2,1)} %bitcast.1), kind=kOutput, calls=%fused_computation.4 | convolution fusion | flops 1258659584 | bytes 7947520 | tf_op jit(solution)/shard_map/dot_general | solution.py:56
  239.5 0.2 convolution_bitcast_fusion
  239.8 102.3 %psum.21 = f32[40]{0:T(128)S(1)} all-reduce(f32[40]{0:T(128)S(1)} %convolution_bitcast_fusion), channel_id=1, replica_groups=mesh['dp'=32,'tensor'=16] {'dp','tensor'}, use_global_device_ids=true, to_apply=%region_1.2 | all-reduce | flops 40 | bytes 320 | tf_op jit(solution)/shard_map/psum | solution.py:73
  342.1 0.0 copy-done.3
  342.1 0.5 multiply_add_fusion.2
  342.6 0.3 convolution_reduce_fusion
  342.9 0.8 multiply_convert_fusion.1
  343.7 0.0 all-gather.5.cloned.1.call-done
  343.7 0.0 copy-done.4
  343.7 10.5 %multiply_reduce_fusion = (f32[864]{0:T(1024)S(1)}, bf16[384,864]{0,1:T(8,128)(2,1)}) fusion(bf16[384,864]{0,1:T(8,128)(2,1)S(1)} %copy-done.4, f32[864]{0:T(1024)S(1)} %get-tuple-element.10, bf16[384,5120]{1,0:T(8,128)(2,1)} %all-gather.3.cloned.1.call-done, bf16[864,5120]{0,1:T(8,128)(2,1)} %all-gather.5.cloned.1.call-done), kind=kOutput, calls=%fused_computation | convolution fusion | flops 3399044352 | bytes 14113536 | tf_op jit(solution)/shard_map/dot_general | solution.py:56
  354.2 46.1 %psum.23 = f32[864]{0:T(1024)S(1)} all-reduce(f32[864]{0:T(1024)S(1)} %get-tuple-element.8), channel_id=1, replica_groups=mesh['dp'=32,'tensor'=16] {'dp'}, use_global_device_ids=true, to_apply=%region_6.7 | all-reduce | flops 864 | bytes 6912 | tf_op jit(solution)/shard_map/psum | solution.py:72
  400.3 0.6 multiply_add_fusion
  (2 shorter events, 0.0 us)
Async XLA Ops:
  7.2 74.5 %all-gather.3.cloned.1.call-start = ((), (), s32[]{:S(2)}) async-start(), calls=%async_computation.1 | async-start | bytes 4177920 | tf_op jit(solution)/shard_map/all_gather | solution.py:52
  7.9 335.8 %all-gather.5.cloned.1.call-start = ((), (), s32[]{:S(2)}) async-start(), calls=%async_computation.2 | async-start | bytes 9461760 | tf_op jit(solution)/shard_map/all_gather | solution.py:63
  11.7 17.0 %copy-start = (f32[864]{0:T(1024)S(1)}, f32[864]{0:T(1024)}, u32[]{:S(2)}) copy-start(f32[864]{0:T(1024)} %param.18) | copy-start | bytes 10372
  11.7 17.0 %copy-start.1 = (f32[864]{0:T(1024)S(1)}, f32[864]{0:T(1024)}, u32[]{:S(2)}) copy-start(f32[864]{0:T(1024)} %param.20) | copy-start | bytes 10372
  11.7 56.1 %copy-start.2 = (f32[40]{0:T(128)S(1)}, f32[40]{0:T(128)}, u32[]{:S(2)}) copy-start(f32[40]{0:T(128)} %param.17) | copy-start | bytes 484
  11.7 222.2 %copy-start.5 = (bf16[384,320]{0,1:T(8,128)(2,1)S(1)}, bf16[384,320]{0,1:T(8,128)(2,1)}, u32[]{:S(2)}) copy-start(bf16[384,320]{0,1:T(8,128)(2,1)} %param.13) | copy-start | bytes 737284
  11.7 222.2 %all-to-all-start = ((bf16[32,320,160]{1,2,0:T(8,128)(2,1)}), bf16[32,320,160]{1,2,0:T(8,128)(2,1)}, u32[]{:S(2)}, u32[]{:S(2)}) async-start(bf16[32,320,160]{1,2,0:T(8,128)(2,1)} %stack.2), calls=%async_computation | async-start | bytes 7864320 | tf_op jit(solution)/shard_map/all_to_all | solution.py:60
  234.0 108.1 %copy-start.3 = (f32[40]{0:T(128)S(1)}, f32[40]{0:T(128)}, u32[]{:S(2)}) copy-start(f32[40]{0:T(128)} %param.19) | copy-start | bytes 484
  234.0 109.7 %copy-start.4 = (bf16[384,864]{0,1:T(8,128)(2,1)S(1)}, bf16[384,864]{0,1:T(8,128)(2,1)}, u32[]{:S(2)}) copy-start(bf16[384,864]{0,1:T(8,128)(2,1)} %param.14) | copy-start | bytes 1990660
Sparse Core Ops, SparseCore 0:
  11.0 70.6 all-gather.2
  83.8 171.4 all-gather.4
